TPU v7x, 32 devices: a whole 2x2x4 slice. The times are simulated.
32 devices in a mesh: grp: 2 (over core), row: 2 (over y), col: 8 (over z, x).
Axes of the slice: x: 2, y: 2, z: 4, core: 2. Of those that a mesh axis runs over, the one named last changes fastest.
Arguments:
- load: float32 [4, 8, 1024, 256], P(('grp', 'row'), 'col'), may hold values from -6 to 6
- guess: float32 [4, 8, 1024, 256], P(('grp', 'row'), 'col'), may hold values from -6 to 6
- interface_op: bfloat16 [4, 8, 1024, 1024], P(('grp', 'row'), 'col'), may hold values from -1 to 5
- precond: bfloat16 [4, 8, 1024, 1024], P(('grp', 'row'), 'col'), may hold values from -1 to 2
- basis: bfloat16 [4, 8, 1024, 64], P(('grp', 'row'), 'col'), may hold values from -0.375 to 0.375
- coarse_inverse: bfloat16 [2048, 2048], P(('grp', 'row'), 'col'), may hold values from -0.1875 to 0.1875
- edge_rows: int32 [4, 8, 1024], P(('grp', 'row'), 'col'), may hold values from 0 to 1023, each once within a row
- coarse_slot: int32 [4, 8, 64], P(('grp', 'row'), 'col'), may hold values from 0 to 63, each once within a row
Outputs:
- displacement: float32 [4, 8, 1024, 256], P(('grp', 'row'), 'col')
Inputs may be any that keep to these rules, and one draw needn't show every extreme that they name: `edge_rows`: each subdomain lists each of its 1024 interface rows once. `coarse_slot`: each subdomain gives each of its 64 basis vectors a different offset.
All inputs are finite; a program needn't handle non-finite values.
Results may differ from a plain program's by a relative error of at most 0.0095.
Values may be sent and summed in bfloat16 or wider, within the bound.
No kernel may reach another device: no remote copies, remote signals or barrier semaphores. Data moves between devices by JAX's collectives and lax.ppermute only.
A program may use at most 64 MiB of HBM per device.

v0:
```python
import jax
import jax.numpy as jnp
from jax import lax
from jax.sharding import PartitionSpec as P

ITERS = 2
OMEGA = 0.6


def extended(shard, sides, width):
    for axis, dim in sides:
        size, length = (lax.axis_size(axis), shard.shape[dim])
        up = [(i, (i + 1) % size) for i in range(size - 1)]
        down = [(j, i) for i, j in up]
        last = lax.slice_in_dim(shard, length - width, length, axis=dim)
        first = lax.slice_in_dim(shard, 0, width, axis=dim)
        before = lax.ppermute(last, axis, up)
        after = lax.ppermute(first, axis, down)
        shard = jnp.concatenate([before, shard, after], axis=dim)
    return shard


def body(load, guess, interface_op, precond, basis, coarse_inverse, edge_rows, coarse_slot):
    local_load = load[0, 0]
    current = guess[0, 0]
    operator_block = interface_op[0, 0]
    precond_block = precond[0, 0]
    basis_block = basis[0, 0]
    row_order = edge_rows[0, 0]
    slot_order = coarse_slot[0, 0]
    n_unknowns, n_cases = local_load.shape
    edge_len = n_unknowns // 4
    n_basis = basis_block.shape[1]
    block_len = coarse_inverse.shape[1]
    grid_rows = lax.axis_size(("grp", "row"))
    grid_cols = lax.axis_size("col")
    my_row = lax.axis_index(("grp", "row"))
    my_col = lax.axis_index("col")
    present = jnp.stack([my_col > 0, my_col < grid_cols - 1, my_row > 0, my_row < grid_rows - 1])
    present = present.astype(jnp.float32)[:, None, None]
    selector = (slot_order[:, None] == jnp.arange(n_basis, dtype=jnp.int32)[None, :]).astype(
        jnp.bfloat16
    )
    contract_first = (((0,), (0,)), ((), ()))

    def place(values):
        blank = jnp.zeros((n_unknowns, n_cases), jnp.float32)
        return blank.at[row_order].set(values.reshape(n_unknowns, n_cases))

    def traces(values):
        own = values[row_order].reshape(4, edge_len, n_cases)
        across_cols = extended(own[0:2], (("col", 0),), 1)
        across_rows = extended(own[2:4], ((("grp", "row"), 0),), 1)
        beside = jnp.stack([across_cols[0], across_cols[3], across_rows[0], across_rows[3]])
        return (own, beside)

    for sweep in range(ITERS):
        applied = jnp.dot(
            operator_block, current.astype(jnp.bfloat16), preferred_element_type=jnp.float32
        )
        own_applied, beside_applied = traces(applied)
        resid = local_load - applied - place(beside_applied)
        resid_bf = resid.astype(jnp.bfloat16)
        local_fix = jnp.dot(precond_block, resid_bf, preferred_element_type=jnp.float32)
        fine_own, fine_beside = traces(local_fix)
        smooth_fix = local_fix + 0.5 * place(present * (fine_beside - fine_own))
        coarse_res = lax.dot_general(
            basis_block, resid_bf, contract_first, preferred_element_type=jnp.float32
        ).astype(jnp.bfloat16)
        ordered = lax.dot_general(
            selector, coarse_res, contract_first, preferred_element_type=jnp.float32
        ).astype(jnp.bfloat16)
        row_block = lax.all_gather(ordered, "col", axis=0, tiled=True)
        source = lax.all_gather(row_block, ("grp", "row"), axis=0, tiled=True)
        offset = my_col * block_len
        column_part = lax.dynamic_slice_in_dim(source, offset, block_len, 0)
        summed = lax.psum_scatter(
            jnp.dot(coarse_inverse, column_part, preferred_element_type=jnp.float32),
            "col",
            scatter_dimension=0,
            tiled=True,
        ).astype(jnp.bfloat16)
        picked = jnp.dot(selector, summed, preferred_element_type=jnp.float32).astype(jnp.bfloat16)
        coarse_fix = jnp.dot(basis_block, picked, preferred_element_type=jnp.float32)
        current = current + OMEGA * (smooth_fix + coarse_fix)
    return current[None, None]


def solution(mesh):
    return jax.shard_map(
        body,
        mesh=mesh,
        in_specs=(
            P(("grp", "row"), "col", None, None),
            P(("grp", "row"), "col", None, None),
            P(("grp", "row"), "col", None, None),
            P(("grp", "row"), "col", None, None),
            P(("grp", "row"), "col", None, None),
            P(("grp", "row"), "col"),
            P(("grp", "row"), "col", None),
            P(("grp", "row"), "col", None),
        ),
        out_specs=P(("grp", "row"), "col", None, None),
        check_vma=False,
    )
```

profile of v0, /device:TPU:0, one launch (start us, length us, event | category | flops | bytes accessed | tf_op | source)
XLA Modules:
  0.0 328.5 jit_solution(16232925203345687816)
XLA Ops:
  10.1 4.7 %gather_fusion = f32[1024,256]{1,0:T(8,128)} fusion(f32[1024,256]{1,0:T(8,128)S(1)} %fusion.6, s32[1024]{0:T(1024)S(1)} %broadcast_clamp_fusion), kind=kCustom, calls=%fused_computation | custom fusion | bytes 2101248 | tf_op jit(solution)/shard_map/gather | solution.py:51
  16.0 4.9 %collective-permute-start = (f32[1,256,256]{2,1,0:T(8,128)S(1)}, f32[1,256,256]{2,1,0:T(8,128)S(1)}, u32[]{:S(2)}, u32[]{:S(2)}) collective-permute-start(f32[1,256,256]{2,1,0:T(8,128)S(1)} %get-tuple-element.17), channel_id=1, source_target_pairs={{0,1},{1,2},{2,3},{3,4},{4,5},{5,6},{6,7},{8,9},{9,10},{10,11},{11... | collective-permute-start | bytes 786440 | tf_op jit(solution)/shard_map/ppermute | solution.py:17
  20.9 3.4 %collective-permute-start.2 = (f32[1,256,256]{2,1,0:T(8,128)S(1)}, f32[1,256,256]{2,1,0:T(8,128)S(1)}, u32[]{:S(2)}, u32[]{:S(2)}) collective-permute-start(f32[1,256,256]{2,1,0:T(8,128)S(1)} %get-tuple-element.18), channel_id=1, source_target_pairs={{0,8},{8,16},{16,24},{1,9},{9,17},{17,25},{2,10},{10,18},{18,26},{... | collective-permute-start | bytes 786440 | tf_op jit(solution)/shard_map/ppermute | solution.py:17
  27.0 4.0 %collective-permute-done.2 = f32[1,256,256]{2,1,0:T(8,128)S(1)} collective-permute-done((f32[1,256,256]{2,1,0:T(8,128)S(1)}, f32[1,256,256]{2,1,0:T(8,128)S(1)}, u32[]{:S(2)}, u32[]{:S(2)}) %collective-permute-start.2) | collective-permute-done | bytes 262176 | tf_op jit(solution)/shard_map/ppermute | solution.py:17
  36.1 6.3 %scatter_custom_fusion = f32[1024,256]{1,0:T(8,128)} fusion(s32[1024]{0:T(1024)S(1)} %bitcast.145, f32[1024,256]{1,0:T(8,128)} %bitcast.140, f32[]{:T(128)} %constant.14.clone.1), kind=kCustom, calls=%fused_computation.58 | custom fusion | bytes 1049088 | tf_op jit(solution)/shard_map/scatter | solution.py:48
  46.3 34.9 %all_gather.12 = bf16[512,256]{1,0:T(8,128)(2,1)} all-gather(bf16[64,256]{1,0:T(8,128)(2,1)S(1)} %convolution_convert_fusion.5), channel_id=1, replica_groups=mesh['grp'=2,'row'=2,'col'=8] {'col'}, dimensions={0}, use_global_device_ids=true | all-gather | bytes 294912 | tf_op jit(solution)/shard_map/all_gather | solution.py:73
  81.2 15.8 %all-gather.3.cloned.1.call-done = bf16[2048,256]{1,0:T(8,128)(2,1)} async-done(((bf16[512,256]{1,0:T(8,128)(2,1)}), bf16[2048,256]{1,0:T(8,128)(2,1)}) %all-gather.3.cloned.1.call-update) | async-done | bytes 1048592 | tf_op jit(solution)/shard_map/all_gather | solution.py:74
  101.7 4.7 %gather_fusion.1 = f32[1024,256]{1,0:T(8,128)} fusion(f32[1024,256]{1,0:T(8,128)S(1)} %fusion.14, s32[1024]{0:T(1024)S(1)} %broadcast_clamp_fusion), kind=kCustom, calls=%fused_computation.1 | custom fusion | bytes 2101248 | tf_op jit(solution)/shard_map/gather | solution.py:51
  107.8 3.4 %collective-permute-start.4 = (f32[1,256,256]{2,1,0:T(8,128)S(1)}, f32[1,256,256]{2,1,0:T(8,128)S(1)}, u32[]{:S(2)}, u32[]{:S(2)}) collective-permute-start(f32[1,256,256]{2,1,0:T(8,128)S(1)} %get-tuple-element.13), channel_id=1, source_target_pairs={{0,1},{1,2},{2,3},{3,4},{4,5},{5,6},{6,7},{8,9},{9,10},{10,11},{11... | collective-permute-start | bytes 786440 | tf_op jit(solution)/shard_map/ppermute | solution.py:17
  112.5 4.6 %collective-permute-start.6 = (f32[1,256,256]{2,1,0:T(8,128)S(1)}, f32[1,256,256]{2,1,0:T(8,128)S(1)}, u32[]{:S(2)}, u32[]{:S(2)}) collective-permute-start(f32[1,256,256]{2,1,0:T(8,128)S(1)} %get-tuple-element.15), channel_id=1, source_target_pairs={{0,8},{8,16},{16,24},{1,9},{9,17},{17,25},{2,10},{10,18},{18,26},{... | collective-permute-start | bytes 786440 | tf_op jit(solution)/shard_map/ppermute | solution.py:17
  122.5 4.4 %collective-permute-done.5 = f32[1,256,256]{2,1,0:T(8,128)S(1)} collective-permute-done((f32[1,256,256]{2,1,0:T(8,128)S(1)}, f32[1,256,256]{2,1,0:T(8,128)S(1)}, u32[]{:S(2)}, u32[]{:S(2)}) %collective-permute-start.5) | collective-permute-done | bytes 262176 | tf_op jit(solution)/shard_map/ppermute | solution.py:18
  128.2 6.3 %scatter_custom_fusion.1 = f32[1024,256]{1,0:T(8,128)} fusion(s32[1024]{0:T(1024)S(1)} %bitcast.146, f32[1024,256]{1,0:T(8,128)} %fusion.25, f32[]{:T(128)} %constant.14.clone.1), kind=kCustom, calls=%fused_computation.56 | custom fusion | bytes 1049088 | tf_op jit(solution)/shard_map/scatter | solution.py:48
  134.5 28.8 %reduce-scatter.7.cloned.1.call-done = f32[64,256]{1,0:T(8,128)} async-done(((f32[512,256]{1,0:T(8,128)}), f32[64,256]{1,0:T(8,128)}) %reduce-scatter.7.cloned.1.call-update) | async-done | bytes 65552
  169.8 4.7 %gather_fusion.2 = f32[1024,256]{1,0:T(8,128)} fusion(f32[1024,256]{1,0:T(8,128)S(1)} %fusion.8, s32[1024]{0:T(1024)S(1)} %broadcast_clamp_fusion), kind=kCustom, calls=%fused_computation.2 | custom fusion | bytes 2101248 | tf_op jit(solution)/shard_map/gather | solution.py:51
  178.9 3.4 %collective-permute-start.10 = (f32[1,256,256]{2,1,0:T(8,128)S(1)}, f32[1,256,256]{2,1,0:T(8,128)S(1)}, u32[]{:S(2)}, u32[]{:S(2)}) collective-permute-start(f32[1,256,256]{2,1,0:T(8,128)S(1)} %get-tuple-element.10), channel_id=1, source_target_pairs={{0,8},{8,16},{16,24},{1,9},{9,17},{17,25},{2,10},{10,18},{18,26},{... | collective-permute-start | bytes 786440 | tf_op jit(solution)/shard_map/ppermute | solution.py:17
  186.3 4.3 %collective-permute-done.9 = f32[1,256,256]{2,1,0:T(8,128)S(1)} collective-permute-done((f32[1,256,256]{2,1,0:T(8,128)S(1)}, f32[1,256,256]{2,1,0:T(8,128)S(1)}, u32[]{:S(2)}, u32[]{:S(2)}) %collective-permute-start.9) | collective-permute-done | bytes 262176 | tf_op jit(solution)/shard_map/ppermute | solution.py:18
  193.3 6.3 %scatter_custom_fusion.2 = f32[1024,256]{1,0:T(8,128)} fusion(s32[1024]{0:T(1024)S(1)} %bitcast.147, f32[1024,256]{1,0:T(8,128)} %bitcast.141, f32[]{:T(128)} %constant.14.clone.1), kind=kCustom, calls=%fused_computation.54 | custom fusion | bytes 1049088 | tf_op jit(solution)/shard_map/scatter | solution.py:48
  203.4 33.6 %all_gather.14 = bf16[512,256]{1,0:T(8,128)(2,1)} all-gather(bf16[64,256]{1,0:T(8,128)(2,1)S(1)} %convolution_convert_fusion.3), channel_id=1, replica_groups=mesh['grp'=2,'row'=2,'col'=8] {'col'}, dimensions={0}, use_global_device_ids=true | all-gather | bytes 294912 | tf_op jit(solution)/shard_map/all_gather | solution.py:73
  237.2 14.9 %all-gather.5.cloned.1.call-done = bf16[2048,256]{1,0:T(8,128)(2,1)} async-done(((bf16[512,256]{1,0:T(8,128)(2,1)}), bf16[2048,256]{1,0:T(8,128)(2,1)}) %all-gather.5.cloned.1.call-update) | async-done | bytes 1048592 | tf_op jit(solution)/shard_map/all_gather | solution.py:74
  256.6 4.7 %gather_fusion.3 = f32[1024,256]{1,0:T(8,128)} fusion(f32[1024,256]{1,0:T(8,128)S(1)} %fusion.11, s32[1024]{0:T(1024)S(1)} %broadcast_clamp_fusion), kind=kCustom, calls=%fused_computation.3 | custom fusion | bytes 2101248 | tf_op jit(solution)/shard_map/gather | solution.py:51
  267.4 4.6 %collective-permute-start.14 = (f32[1,256,256]{2,1,0:T(8,128)S(1)}, f32[1,256,256]{2,1,0:T(8,128)S(1)}, u32[]{:S(2)}, u32[]{:S(2)}) collective-permute-start(f32[1,256,256]{2,1,0:T(8,128)S(1)} %get-tuple-element.7), channel_id=1, source_target_pairs={{0,8},{8,16},{16,24},{1,9},{9,17},{17,25},{2,10},{10,18},{18,26},{... | collective-permute-start | bytes 786440 | tf_op jit(solution)/shard_map/ppermute | solution.py:17
  277.5 4.4 %collective-permute-done.13 = f32[1,256,256]{2,1,0:T(8,128)S(1)} collective-permute-done((f32[1,256,256]{2,1,0:T(8,128)S(1)}, f32[1,256,256]{2,1,0:T(8,128)S(1)}, u32[]{:S(2)}, u32[]{:S(2)}) %collective-permute-start.13) | collective-permute-done | bytes 262176 | tf_op jit(solution)/shard_map/ppermute | solution.py:18
  283.1 6.3 %scatter_custom_fusion.3 = f32[1024,256]{1,0:T(8,128)} fusion(s32[1024]{0:T(1024)S(1)} %bitcast.148, f32[1024,256]{1,0:T(8,128)} %fusion.24, f32[]{:T(128)} %constant.14.clone.1), kind=kCustom, calls=%fused_computation.52 | custom fusion | bytes 1049088 | tf_op jit(solution)/shard_map/scatter | solution.py:48
  289.4 28.6 %reduce-scatter.9.cloned.1.call-done = f32[64,256]{1,0:T(8,128)} async-done(((f32[512,256]{1,0:T(8,128)}), f32[64,256]{1,0:T(8,128)}) %reduce-scatter.9.cloned.1.call-update) | async-done | bytes 65552
  (73 shorter events, 73.4 us)
Async XLA Ops:
  6.5 90.5 %all-gather.3.cloned.1.call-start = ((), (), s32[]{:S(2)}) async-start(), calls=%async_computation.2 | async-start | bytes 1310720 | tf_op jit(solution)/shard_map/all_gather | solution.py:74
  16.0 10.9 %collective-permute-start = (f32[1,256,256]{2,1,0:T(8,128)S(1)}, f32[1,256,256]{2,1,0:T(8,128)S(1)}, u32[]{:S(2)}, u32[]{:S(2)}) collective-permute-start(f32[1,256,256]{2,1,0:T(8,128)S(1)} %get-tuple-element.17), channel_id=1, source_target_pairs={{0,1},{1,2},{2,3},{3,4},{4,5},{5,6},{6,7},{8,9},{9,10},{10,11},{11... | collective-permute-start | bytes 786440 | tf_op jit(solution)/shard_map/ppermute | solution.py:17
  20.9 10.1 %collective-permute-start.2 = (f32[1,256,256]{2,1,0:T(8,128)S(1)}, f32[1,256,256]{2,1,0:T(8,128)S(1)}, u32[]{:S(2)}, u32[]{:S(2)}) collective-permute-start(f32[1,256,256]{2,1,0:T(8,128)S(1)} %get-tuple-element.18), channel_id=1, source_target_pairs={{0,8},{8,16},{16,24},{1,9},{9,17},{17,25},{2,10},{10,18},{18,26},{... | collective-permute-start | bytes 786440 | tf_op jit(solution)/shard_map/ppermute | solution.py:17
  24.4 9.4 %collective-permute-start.1 = (f32[1,256,256]{2,1,0:T(8,128)S(1)}, f32[1,256,256]{2,1,0:T(8,128)S(1)}, u32[]{:S(2)}, u32[]{:S(2)}) collective-permute-start(f32[1,256,256]{2,1,0:T(8,128)S(1)} %get-tuple-element.19), channel_id=1, source_target_pairs={{1,0},{2,1},{3,2},{4,3},{5,4},{6,5},{7,6},{9,8},{10,9},{11,10},{12... | collective-permute-start | bytes 786440 | tf_op jit(solution)/shard_map/ppermute | solution.py:18
  25.7 9.4 %collective-permute-start.3 = (f32[1,256,256]{2,1,0:T(8,128)S(1)}, f32[1,256,256]{2,1,0:T(8,128)S(1)}, u32[]{:S(2)}, u32[]{:S(2)}) collective-permute-start(f32[1,256,256]{2,1,0:T(8,128)S(1)} %get-tuple-element.20), channel_id=1, source_target_pairs={{8,0},{16,8},{24,16},{9,1},{17,9},{25,17},{10,2},{18,10},{26,18},{... | collective-permute-start | bytes 786440 | tf_op jit(solution)/shard_map/ppermute | solution.py:18
  42.4 2.6 copy-start.5
  42.4 54.7 %copy-start.4 = (bf16[512,256]{1,0:T(8,128)(2,1)S(1)}, bf16[512,256]{1,0:T(8,128)(2,1)}, u32[]{:S(2)}) copy-start(bf16[512,256]{1,0:T(8,128)(2,1)} %param.13) | copy-start | bytes 786436
  81.2 82.1 %reduce-scatter.7.cloned.1.call-start = ((), (), s32[]{:S(2)}) async-start(), calls=%async_computation.4 | async-start | bytes 589824
  99.3 152.8 %all-gather.5.cloned.1.call-start = ((), (), s32[]{:S(2)}) async-start(), calls=%async_computation.3 | async-start | bytes 1310720 | tf_op jit(solution)/shard_map/all_gather | solution.py:74
  106.4 20.6 %copy-start.1 = (f32[1024,256]{1,0:T(8,128)S(1)}, f32[1024,256]{1,0:T(8,128)}, u32[]{:S(2)}) copy-start(f32[1024,256]{1,0:T(8,128)} %gather_fusion.1) | copy-start | bytes 3145732
  107.8 10.7 %collective-permute-start.4 = (f32[1,256,256]{2,1,0:T(8,128)S(1)}, f32[1,256,256]{2,1,0:T(8,128)S(1)}, u32[]{:S(2)}, u32[]{:S(2)}) collective-permute-start(f32[1,256,256]{2,1,0:T(8,128)S(1)} %get-tuple-element.13), channel_id=1, source_target_pairs={{0,1},{1,2},{2,3},{3,4},{4,5},{5,6},{6,7},{8,9},{9,10},{10,11},{11... | collective-permute-start | bytes 786440 | tf_op jit(solution)/shard_map/ppermute | solution.py:17
  111.2 10.0 %collective-permute-start.7 = (f32[1,256,256]{2,1,0:T(8,128)S(1)}, f32[1,256,256]{2,1,0:T(8,128)S(1)}, u32[]{:S(2)}, u32[]{:S(2)}) collective-permute-start(f32[1,256,256]{2,1,0:T(8,128)S(1)} %get-tuple-element.14), channel_id=1, source_target_pairs={{8,0},{16,8},{24,16},{9,1},{17,9},{25,17},{10,2},{18,10},{26,18},{... | collective-permute-start | bytes 786440 | tf_op jit(solution)/shard_map/ppermute | solution.py:18
  112.5 10.1 %collective-permute-start.6 = (f32[1,256,256]{2,1,0:T(8,128)S(1)}, f32[1,256,256]{2,1,0:T(8,128)S(1)}, u32[]{:S(2)}, u32[]{:S(2)}) collective-permute-start(f32[1,256,256]{2,1,0:T(8,128)S(1)} %get-tuple-element.15), channel_id=1, source_target_pairs={{0,8},{8,16},{16,24},{1,9},{9,17},{17,25},{2,10},{10,18},{18,26},{... | collective-permute-start | bytes 786440 | tf_op jit(solution)/shard_map/ppermute | solution.py:17
  117.0 9.9 %collective-permute-start.5 = (f32[1,256,256]{2,1,0:T(8,128)S(1)}, f32[1,256,256]{2,1,0:T(8,128)S(1)}, u32[]{:S(2)}, u32[]{:S(2)}) collective-permute-start(f32[1,256,256]{2,1,0:T(8,128)S(1)} %get-tuple-element.16), channel_id=1, source_target_pairs={{1,0},{2,1},{3,2},{4,3},{5,4},{6,5},{7,6},{9,8},{10,9},{11,10},{12... | collective-permute-start | bytes 786440 | tf_op jit(solution)/shard_map/ppermute | solution.py:18
  175.7 9.4 %collective-permute-start.8 = (f32[1,256,256]{2,1,0:T(8,128)S(1)}, f32[1,256,256]{2,1,0:T(8,128)S(1)}, u32[]{:S(2)}, u32[]{:S(2)}) collective-permute-start(f32[1,256,256]{2,1,0:T(8,128)S(1)} %get-tuple-element.9), channel_id=1, source_target_pairs={{0,1},{1,2},{2,3},{3,4},{4,5},{5,6},{6,7},{8,9},{9,10},{10,11},{11... | collective-permute-start | bytes 786440 | tf_op jit(solution)/shard_map/ppermute | solution.py:17
  178.9 7.4 %collective-permute-start.10 = (f32[1,256,256]{2,1,0:T(8,128)S(1)}, f32[1,256,256]{2,1,0:T(8,128)S(1)}, u32[]{:S(2)}, u32[]{:S(2)}) collective-permute-start(f32[1,256,256]{2,1,0:T(8,128)S(1)} %get-tuple-element.10), channel_id=1, source_target_pairs={{0,8},{8,16},{16,24},{1,9},{9,17},{17,25},{2,10},{10,18},{18,26},{... | collective-permute-start | bytes 786440 | tf_op jit(solution)/shard_map/ppermute | solution.py:17
  182.3 8.3 %collective-permute-start.9 = (f32[1,256,256]{2,1,0:T(8,128)S(1)}, f32[1,256,256]{2,1,0:T(8,128)S(1)}, u32[]{:S(2)}, u32[]{:S(2)}) collective-permute-start(f32[1,256,256]{2,1,0:T(8,128)S(1)} %get-tuple-element.11), channel_id=1, source_target_pairs={{1,0},{2,1},{3,2},{4,3},{5,4},{6,5},{7,6},{9,8},{10,9},{11,10},{12... | collective-permute-start | bytes 786440 | tf_op jit(solution)/shard_map/ppermute | solution.py:18
  183.6 8.6 %collective-permute-start.11 = (f32[1,256,256]{2,1,0:T(8,128)S(1)}, f32[1,256,256]{2,1,0:T(8,128)S(1)}, u32[]{:S(2)}, u32[]{:S(2)}) collective-permute-start(f32[1,256,256]{2,1,0:T(8,128)S(1)} %get-tuple-element.12), channel_id=1, source_target_pairs={{8,0},{16,8},{24,16},{9,1},{17,9},{25,17},{10,2},{18,10},{26,18},{... | collective-permute-start | bytes 786440 | tf_op jit(solution)/shard_map/ppermute | solution.py:18
  237.1 80.9 %reduce-scatter.9.cloned.1.call-start = ((), (), s32[]{:S(2)}) async-start(), calls=%async_computation.5 | async-start | bytes 589824
  261.3 20.6 %copy-start.2 = (f32[1024,256]{1,0:T(8,128)S(1)}, f32[1024,256]{1,0:T(8,128)}, u32[]{:S(2)}) copy-start(f32[1024,256]{1,0:T(8,128)} %gather_fusion.3) | copy-start | bytes 3145732
  262.7 10.5 %collective-permute-start.12 = (f32[1,256,256]{2,1,0:T(8,128)S(1)}, f32[1,256,256]{2,1,0:T(8,128)S(1)}, u32[]{:S(2)}, u32[]{:S(2)}) collective-permute-start(f32[1,256,256]{2,1,0:T(8,128)S(1)} %get-tuple-element.5), channel_id=1, source_target_pairs={{0,1},{1,2},{2,3},{3,4},{4,5},{5,6},{6,7},{8,9},{9,10},{10,11},{11... | collective-permute-start | bytes 786440 | tf_op jit(solution)/shard_map/ppermute | solution.py:17
  266.1 10.1 %collective-permute-start.15 = (f32[1,256,256]{2,1,0:T(8,128)S(1)}, f32[1,256,256]{2,1,0:T(8,128)S(1)}, u32[]{:S(2)}, u32[]{:S(2)}) collective-permute-start(f32[1,256,256]{2,1,0:T(8,128)S(1)} %get-tuple-element.6), channel_id=1, source_target_pairs={{8,0},{16,8},{24,16},{9,1},{17,9},{25,17},{10,2},{18,10},{26,18},{... | collective-permute-start | bytes 786440 | tf_op jit(solution)/shard_map/ppermute | solution.py:18
  267.4 10.1 %collective-permute-start.14 = (f32[1,256,256]{2,1,0:T(8,128)S(1)}, f32[1,256,256]{2,1,0:T(8,128)S(1)}, u32[]{:S(2)}, u32[]{:S(2)}) collective-permute-start(f32[1,256,256]{2,1,0:T(8,128)S(1)} %get-tuple-element.7), channel_id=1, source_target_pairs={{0,8},{8,16},{16,24},{1,9},{9,17},{17,25},{2,10},{10,18},{18,26},{... | collective-permute-start | bytes 786440 | tf_op jit(solution)/shard_map/ppermute | solution.py:17
  271.9 9.9 %collective-permute-start.13 = (f32[1,256,256]{2,1,0:T(8,128)S(1)}, f32[1,256,256]{2,1,0:T(8,128)S(1)}, u32[]{:S(2)}, u32[]{:S(2)}) collective-permute-start(f32[1,256,256]{2,1,0:T(8,128)S(1)} %get-tuple-element.8), channel_id=1, source_target_pairs={{1,0},{2,1},{3,2},{4,3},{5,4},{6,5},{7,6},{9,8},{10,9},{11,10},{12... | collective-permute-start | bytes 786440 | tf_op jit(solution)/shard_map/ppermute | solution.py:18
  (2 other events, 4.2 us)
Sparse Core Ops, SparseCore 0:
  81.3 15.7 all-gather.2
  100.4 62.7 reduce-scatter.6
  237.2 14.7 all-gather.4
  255.2 62.7 reduce-scatter.8
where the time goes:
time: 330 us; the launch traced here: 329 us
  waiting for transfers between devices  120 us (36%)
  blocking collectives  68.5 us (21%)
  local copies, waits for them, and re-layouts  54.5 us (17%)
  starting transfers between devices  41.4 us (13%)
  matrix products  19.8 us (6%)
  between operations  13.4 us (4%)
  other arithmetic  10.5 us (3%)
    all_gather x2, blocking collectives, body(): row_block = lax.all_gather(ordered, 'col', axis=0, tiled=True)  68.5 us
    unnamed x6, waiting for transfers between devices  57.4 us
    ppermute x8, starting transfers between devices, extended(): before = lax.ppermute(last, axis, up)  30.8 us
    all_gather x2, waiting for transfers between devices, body(): source = lax.all_gather(row_block, ('grp', 'row'), axis=0, tiled=True)  30.7 us
    scatter x4, local copies, waits for them, and re-layouts, place(): return blank.at[row_order].set(values.reshape(n_unknowns, n_cases))  25.1 us
    ppermute x8, waiting for transfers between devices, extended(): after = lax.ppermute(first, axis, down)  24.3 us
    gather x4, local copies, waits for them, and re-layouts, traces(): own = values[row_order].reshape(4, edge_len, n_cases)  18.7 us
    ppermute x8, starting transfers between devices, extended(): after = lax.ppermute(first, axis, down)  10.5 us
  transfers between devices with their start and end apart: 20, of which 16 were waited for; matrix products, arithmetic and copies ran while one was open for 10% of the time, Pallas kernels for 0%

commit v1 on v0

--- a/solution.py
+++ b/solution.py
@@ -5,6 +5,28 @@
 
 ITERS = 2
 OMEGA = 0.6
+
+
+def in_order(tiles, dim):
+    tiles = jnp.moveaxis(tiles, 0, dim)
+    lengths = tiles.shape
+    return tiles.reshape(*lengths[:dim], lengths[dim] * lengths[dim + 1], *lengths[dim + 2 :])
+
+
+def collect(x, axis, dim):
+    size = lax.axis_size(axis)
+    pairs = [(i, (i + 1) % size) for i in range(size)]
+    back = [(b, a) for a, b in pairs]
+    lower, upper = ([], [])
+    for step in range(size - 1):
+        if step % 2 == 0:
+            lower.append(lax.ppermute(lower[-1] if lower else x, axis, pairs))
+        else:
+            upper.append(lax.ppermute(upper[-1] if upper else x, axis, back))
+    tiles = jnp.stack([*lower[::-1], x, *upper])
+    shift = lax.axis_index(axis) - len(lower)
+    tiles = tiles[(jnp.arange(size) - shift) % size]
+    return in_order(tiles, dim)
 
 
 def extended(shard, sides, width):
@@ -70,7 +92,7 @@
         ordered = lax.dot_general(
             selector, coarse_res, contract_first, preferred_element_type=jnp.float32
         ).astype(jnp.bfloat16)
-        row_block = lax.all_gather(ordered, "col", axis=0, tiled=True)
+        row_block = collect(ordered, "col", 0)
         source = lax.all_gather(row_block, ("grp", "row"), axis=0, tiled=True)
         offset = my_col * block_len
         column_part = lax.dynamic_slice_in_dim(source, offset, block_len, 0)

time: 330 us -> 322 us (0.976)
  blocking collectives: 68.5 us -> 0 us
  starting transfers between devices: 41.4 us -> 74.6 us
  waiting for transfers between devices: 120 us -> 145 us
    all_gather x2 -> x0, blocking collectives: 68.5 us -> none  [body(): row_block = lax.all_gather(ordered, 'col', axis=0, tiled=True)]
    ppermute x0 -> x14, starting transfers between devices: none -> 33.2 us  [the longest x6 28.5 us: collect(): upper.append(lax.ppermute(upper[-1] if upper else x, axis, back))]
    ppermute x0 -> x14, waiting for transfers between devices: none -> 20.6 us  [the longest x8 20.6 us: collect(): lower.append(lax.ppermute(lower[-1] if lower else x, axis, pairs))]
    all_gather x2, waiting for transfers between devices: 30.7 us -> 34.6 us  [body(): source = lax.all_gather(row_block, ('grp', 'row'), axis=0, tiled=True)]
  transfers between devices with their start and end apart: 20 -> 34, of which waited for: 16 -> 24; matrix products, arithmetic and copies ran while one was open for 10% -> 10% of each run, Pallas kernels for 0% -> 0%
where the time goes in v1:
time: 322 us; the launch traced here: 320 us
  waiting for transfers between devices  145 us (45%)
  starting transfers between devices  74.6 us (23%)
  local copies, waits for them, and re-layouts  57.1 us (18%)
  matrix products  19.7 us (6%)
  between operations  13.6 us (4%)
  other arithmetic  10.6 us (3%)
    unnamed x6, waiting for transfers between devices  57.4 us
    all_gather x2, waiting for transfers between devices, body(): source = lax.all_gather(row_block, ('grp', 'row'), axis=0, tiled=True)  34.6 us
    ppermute x8, starting transfers between devices, extended(): before = lax.ppermute(last, axis, up)  30.8 us
    ppermute x6, starting transfers between devices, collect(): upper.append(lax.ppermute(upper[-1] if upper else x, axis, back))  28.5 us
    scatter x4, local copies, waits for them, and re-layouts, place(): return blank.at[row_order].set(values.reshape(n_unknowns, n_cases))  25.1 us
    ppermute x8, waiting for transfers between devices, extended(): after = lax.ppermute(first, axis, down)  24.4 us
    ppermute x8, waiting for transfers between devices, collect(): lower.append(lax.ppermute(lower[-1] if lower else x, axis, pairs))  20.6 us
    gather x4, local copies, waits for them, and re-layouts, traces(): own = values[row_order].reshape(4, edge_len, n_cases)  18.7 us
  transfers between devices with their start and end apart: 34, of which 24 were waited for; matrix products, arithmetic and copies ran while one was open for 10% of the time, Pallas kernels for 0%

profile of v1, /device:TPU:0, one launch (start us, length us, event | category | flops | bytes accessed | tf_op | source)
XLA Modules:
  0.0 320.5 jit_solution(5504414193921873513)
XLA Ops:
  10.1 4.7 %gather_fusion = f32[1024,256]{1,0:T(8,128)} fusion(f32[1024,256]{1,0:T(8,128)S(1)} %fusion.6, s32[1024]{0:T(1024)S(1)} %broadcast_clamp_fusion), kind=kCustom, calls=%fused_computation | custom fusion | bytes 2101248 | tf_op jit(solution)/shard_map/gather | solution.py:73
  16.0 4.9 %collective-permute-start = (f32[1,256,256]{2,1,0:T(8,128)S(1)}, f32[1,256,256]{2,1,0:T(8,128)S(1)}, u32[]{:S(2)}, u32[]{:S(2)}) collective-permute-start(f32[1,256,256]{2,1,0:T(8,128)S(1)} %get-tuple-element.17), channel_id=1, source_target_pairs={{0,1},{1,2},{2,3},{3,4},{4,5},{5,6},{6,7},{8,9},{9,10},{10,11},{11... | collective-permute-start | bytes 786440 | tf_op jit(solution)/shard_map/ppermute | solution.py:39
  36.1 6.3 %scatter_custom_fusion = f32[1024,256]{1,0:T(8,128)} fusion(s32[1024]{0:T(1024)S(1)} %bitcast.183, f32[1024,256]{1,0:T(8,128)} %bitcast.178, f32[]{:T(128)} %constant.17.clone.1), kind=kCustom, calls=%fused_computation.60 | custom fusion | bytes 1049088 | tf_op jit(solution)/shard_map/scatter | solution.py:70
  48.7 4.9 %collective-permute-done.8 = bf16[64,256]{1,0:T(8,128)(2,1)S(1)} collective-permute-done((bf16[64,256]{1,0:T(8,128)(2,1)S(1)}, bf16[64,256]{1,0:T(8,128)(2,1)S(1)}, u32[]{:S(2)}, u32[]{:S(2)}) %collective-permute-start.8) | collective-permute-done | bytes 32800 | tf_op jit(solution)/shard_map/ppermute | solution.py:23
  53.6 4.7 %collective-permute-start.12 = (bf16[64,256]{1,0:T(8,128)(2,1)S(1)}, bf16[64,256]{1,0:T(8,128)(2,1)S(1)}, u32[]{:S(2)}, u32[]{:S(2)}) collective-permute-start(bf16[64,256]{1,0:T(8,128)(2,1)S(1)} %convolution_convert_fusion.5), channel_id=1, source_target_pairs={{1,0},{2,1},{3,2},{4,3},{5,4},{6,5},{7,6},{0,7},{9,8},{10,9},{11,1... | collective-permute-start | bytes 98312 | tf_op jit(solution)/shard_map/ppermute | solution.py:25
  60.2 4.8 %collective-permute-start.13 = (bf16[64,256]{1,0:T(8,128)(2,1)S(1)}, bf16[64,256]{1,0:T(8,128)(2,1)S(1)}, u32[]{:S(2)}, u32[]{:S(2)}) collective-permute-start(bf16[64,256]{1,0:T(8,128)(2,1)S(1)} %collective-permute-done.12), channel_id=1, source_target_pairs={{1,0},{2,1},{3,2},{4,3},{5,4},{6,5},{7,6},{0,7},{9,8},{10,9},{11,1... | collective-permute-start | bytes 98312 | tf_op jit(solution)/shard_map/ppermute | solution.py:25
  66.9 4.9 %collective-permute-start.14 = (bf16[64,256]{1,0:T(8,128)(2,1)S(1)}, bf16[64,256]{1,0:T(8,128)(2,1)S(1)}, u32[]{:S(2)}, u32[]{:S(2)}) collective-permute-start(bf16[64,256]{1,0:T(8,128)(2,1)S(1)} %collective-permute-done.13), channel_id=1, source_target_pairs={{1,0},{2,1},{3,2},{4,3},{5,4},{6,5},{7,6},{0,7},{9,8},{10,9},{11,1... | collective-permute-start | bytes 98312 | tf_op jit(solution)/shard_map/ppermute | solution.py:25
  74.9 17.4 %all-gather.3.cloned.1.call-done = bf16[2048,256]{1,0:T(8,128)(2,1)} async-done(((bf16[512,256]{1,0:T(8,128)(2,1)}), bf16[2048,256]{1,0:T(8,128)(2,1)}) %all-gather.3.cloned.1.call-update) | async-done | bytes 1048592 | tf_op jit(solution)/shard_map/all_gather | solution.py:96
  96.9 4.7 %gather_fusion.1 = f32[1024,256]{1,0:T(8,128)} fusion(f32[1024,256]{1,0:T(8,128)S(1)} %fusion.14, s32[1024]{0:T(1024)S(1)} %broadcast_clamp_fusion), kind=kCustom, calls=%fused_computation.1 | custom fusion | bytes 2101248 | tf_op jit(solution)/shard_map/gather | solution.py:73
  107.6 4.6 %collective-permute-start.6 = (f32[1,256,256]{2,1,0:T(8,128)S(1)}, f32[1,256,256]{2,1,0:T(8,128)S(1)}, u32[]{:S(2)}, u32[]{:S(2)}) collective-permute-start(f32[1,256,256]{2,1,0:T(8,128)S(1)} %get-tuple-element.15), channel_id=1, source_target_pairs={{0,8},{8,16},{16,24},{1,9},{9,17},{17,25},{2,10},{10,18},{18,26},{... | collective-permute-start | bytes 786440 | tf_op jit(solution)/shard_map/ppermute | solution.py:39
  123.4 6.3 %scatter_custom_fusion.1 = f32[1024,256]{1,0:T(8,128)} fusion(s32[1024]{0:T(1024)S(1)} %bitcast.184, f32[1024,256]{1,0:T(8,128)} %fusion.25, f32[]{:T(128)} %constant.17.clone.1), kind=kCustom, calls=%fused_computation.58 | custom fusion | bytes 1049088 | tf_op jit(solution)/shard_map/scatter | solution.py:70
  129.6 28.8 %reduce-scatter.7.cloned.1.call-done = f32[64,256]{1,0:T(8,128)} async-done(((f32[512,256]{1,0:T(8,128)}), f32[64,256]{1,0:T(8,128)}) %reduce-scatter.7.cloned.1.call-update) | async-done | bytes 65552
  164.9 4.7 %gather_fusion.3 = f32[1024,256]{1,0:T(8,128)} fusion(f32[1024,256]{1,0:T(8,128)S(1)} %fusion.8, s32[1024]{0:T(1024)S(1)} %broadcast_clamp_fusion), kind=kCustom, calls=%fused_computation.3 | custom fusion | bytes 2101248 | tf_op jit(solution)/shard_map/gather | solution.py:73
  188.5 6.3 %scatter_custom_fusion.2 = f32[1024,256]{1,0:T(8,128)} fusion(s32[1024]{0:T(1024)S(1)} %bitcast.185, f32[1024,256]{1,0:T(8,128)} %bitcast.179, f32[]{:T(128)} %constant.17.clone.1), kind=kCustom, calls=%fused_computation.56 | custom fusion | bytes 1049088 | tf_op jit(solution)/shard_map/scatter | solution.py:70
  200.9 4.4 %collective-permute-done.23 = bf16[64,256]{1,0:T(8,128)(2,1)S(1)} collective-permute-done((bf16[64,256]{1,0:T(8,128)(2,1)S(1)}, bf16[64,256]{1,0:T(8,128)(2,1)S(1)}, u32[]{:S(2)}, u32[]{:S(2)}) %collective-permute-start.23) | collective-permute-done | bytes 32800 | tf_op jit(solution)/shard_map/ppermute | solution.py:23
  205.3 4.7 %collective-permute-start.27 = (bf16[64,256]{1,0:T(8,128)(2,1)S(1)}, bf16[64,256]{1,0:T(8,128)(2,1)S(1)}, u32[]{:S(2)}, u32[]{:S(2)}) collective-permute-start(bf16[64,256]{1,0:T(8,128)(2,1)S(1)} %convolution_convert_fusion.3), channel_id=1, source_target_pairs={{1,0},{2,1},{3,2},{4,3},{5,4},{6,5},{7,6},{0,7},{9,8},{10,9},{11,1... | collective-permute-start | bytes 98312 | tf_op jit(solution)/shard_map/ppermute | solution.py:25
  211.9 4.7 %collective-permute-start.28 = (bf16[64,256]{1,0:T(8,128)(2,1)S(1)}, bf16[64,256]{1,0:T(8,128)(2,1)S(1)}, u32[]{:S(2)}, u32[]{:S(2)}) collective-permute-start(bf16[64,256]{1,0:T(8,128)(2,1)S(1)} %collective-permute-done.27), channel_id=1, source_target_pairs={{1,0},{2,1},{3,2},{4,3},{5,4},{6,5},{7,6},{0,7},{9,8},{10,9},{11,1... | collective-permute-start | bytes 98312 | tf_op jit(solution)/shard_map/ppermute | solution.py:25
  218.7 4.7 %collective-permute-start.29 = (bf16[64,256]{1,0:T(8,128)(2,1)S(1)}, bf16[64,256]{1,0:T(8,128)(2,1)S(1)}, u32[]{:S(2)}, u32[]{:S(2)}) collective-permute-start(bf16[64,256]{1,0:T(8,128)(2,1)S(1)} %collective-permute-done.28), channel_id=1, source_target_pairs={{1,0},{2,1},{3,2},{4,3},{5,4},{6,5},{7,6},{0,7},{9,8},{10,9},{11,1... | collective-permute-start | bytes 98312 | tf_op jit(solution)/shard_map/ppermute | solution.py:25
  226.8 17.2 %all-gather.5.cloned.1.call-done = bf16[2048,256]{1,0:T(8,128)(2,1)} async-done(((bf16[512,256]{1,0:T(8,128)(2,1)}), bf16[2048,256]{1,0:T(8,128)(2,1)}) %all-gather.5.cloned.1.call-update) | async-done | bytes 1048592 | tf_op jit(solution)/shard_map/all_gather | solution.py:96
  248.6 4.7 %gather_fusion.4 = f32[1024,256]{1,0:T(8,128)} fusion(f32[1024,256]{1,0:T(8,128)S(1)} %fusion.11, s32[1024]{0:T(1024)S(1)} %broadcast_clamp_fusion), kind=kCustom, calls=%fused_computation.4 | custom fusion | bytes 2101248 | tf_op jit(solution)/shard_map/gather | solution.py:73
  259.3 4.6 %collective-permute-start.21 = (f32[1,256,256]{2,1,0:T(8,128)S(1)}, f32[1,256,256]{2,1,0:T(8,128)S(1)}, u32[]{:S(2)}, u32[]{:S(2)}) collective-permute-start(f32[1,256,256]{2,1,0:T(8,128)S(1)} %get-tuple-element.7), channel_id=1, source_target_pairs={{0,8},{8,16},{16,24},{1,9},{9,17},{17,25},{2,10},{10,18},{18,26},{... | collective-permute-start | bytes 786440 | tf_op jit(solution)/shard_map/ppermute | solution.py:39
  269.4 4.4 %collective-permute-done.20 = f32[1,256,256]{2,1,0:T(8,128)S(1)} collective-permute-done((f32[1,256,256]{2,1,0:T(8,128)S(1)}, f32[1,256,256]{2,1,0:T(8,128)S(1)}, u32[]{:S(2)}, u32[]{:S(2)}) %collective-permute-start.20) | collective-permute-done | bytes 262176 | tf_op jit(solution)/shard_map/ppermute | solution.py:40
  275.1 6.3 %scatter_custom_fusion.3 = f32[1024,256]{1,0:T(8,128)} fusion(s32[1024]{0:T(1024)S(1)} %bitcast.186, f32[1024,256]{1,0:T(8,128)} %fusion.24, f32[]{:T(128)} %constant.17.clone.1), kind=kCustom, calls=%fused_computation.54 | custom fusion | bytes 1049088 | tf_op jit(solution)/shard_map/scatter | solution.py:70
  281.4 28.6 %reduce-scatter.9.cloned.1.call-done = f32[64,256]{1,0:T(8,128)} async-done(((f32[512,256]{1,0:T(8,128)}), f32[64,256]{1,0:T(8,128)}) %reduce-scatter.9.cloned.1.call-update) | async-done | bytes 65552
  (121 shorter events, 114.9 us)
Async XLA Ops:
  6.5 85.7 %all-gather.3.cloned.1.call-start = ((), (), s32[]{:S(2)}) async-start(), calls=%async_computation.2 | async-start | bytes 1310720 | tf_op jit(solution)/shard_map/all_gather | solution.py:96
  16.0 10.9 %collective-permute-start = (f32[1,256,256]{2,1,0:T(8,128)S(1)}, f32[1,256,256]{2,1,0:T(8,128)S(1)}, u32[]{:S(2)}, u32[]{:S(2)}) collective-permute-start(f32[1,256,256]{2,1,0:T(8,128)S(1)} %get-tuple-element.17), channel_id=1, source_target_pairs={{0,1},{1,2},{2,3},{3,4},{4,5},{5,6},{6,7},{8,9},{9,10},{10,11},{11... | collective-permute-start | bytes 786440 | tf_op jit(solution)/shard_map/ppermute | solution.py:39
  20.9 10.1 %collective-permute-start.2 = (f32[1,256,256]{2,1,0:T(8,128)S(1)}, f32[1,256,256]{2,1,0:T(8,128)S(1)}, u32[]{:S(2)}, u32[]{:S(2)}) collective-permute-start(f32[1,256,256]{2,1,0:T(8,128)S(1)} %get-tuple-element.18), channel_id=1, source_target_pairs={{0,8},{8,16},{16,24},{1,9},{9,17},{17,25},{2,10},{10,18},{18,26},{... | collective-permute-start | bytes 786440 | tf_op jit(solution)/shard_map/ppermute | solution.py:39
  24.4 9.4 %collective-permute-start.1 = (f32[1,256,256]{2,1,0:T(8,128)S(1)}, f32[1,256,256]{2,1,0:T(8,128)S(1)}, u32[]{:S(2)}, u32[]{:S(2)}) collective-permute-start(f32[1,256,256]{2,1,0:T(8,128)S(1)} %get-tuple-element.19), channel_id=1, source_target_pairs={{1,0},{2,1},{3,2},{4,3},{5,4},{6,5},{7,6},{9,8},{10,9},{11,10},{12... | collective-permute-start | bytes 786440 | tf_op jit(solution)/shard_map/ppermute | solution.py:40
  25.7 9.4 %collective-permute-start.3 = (f32[1,256,256]{2,1,0:T(8,128)S(1)}, f32[1,256,256]{2,1,0:T(8,128)S(1)}, u32[]{:S(2)}, u32[]{:S(2)}) collective-permute-start(f32[1,256,256]{2,1,0:T(8,128)S(1)} %get-tuple-element.20), channel_id=1, source_target_pairs={{8,0},{16,8},{24,16},{9,1},{17,9},{25,17},{10,2},{18,10},{26,18},{... | collective-permute-start | bytes 786440 | tf_op jit(solution)/shard_map/ppermute | solution.py:40
  46.3 7.3 %collective-permute-start.8 = (bf16[64,256]{1,0:T(8,128)(2,1)S(1)}, bf16[64,256]{1,0:T(8,128)(2,1)S(1)}, u32[]{:S(2)}, u32[]{:S(2)}) collective-permute-start(bf16[64,256]{1,0:T(8,128)(2,1)S(1)} %convolution_convert_fusion.5), channel_id=1, source_target_pairs={{0,1},{1,2},{2,3},{3,4},{4,5},{5,6},{6,7},{7,0},{8,9},{9,10},{10,1... | collective-permute-start | bytes 98312 | tf_op jit(solution)/shard_map/ppermute | solution.py:23
  74.8 83.6 %reduce-scatter.7.cloned.1.call-start = ((), (), s32[]{:S(2)}) async-start(), calls=%async_computation.4 | async-start | bytes 589824
  94.4 149.6 %all-gather.5.cloned.1.call-start = ((), (), s32[]{:S(2)}) async-start(), calls=%async_computation.3 | async-start | bytes 1310720 | tf_op jit(solution)/shard_map/all_gather | solution.py:96
  102.9 10.7 %collective-permute-start.4 = (f32[1,256,256]{2,1,0:T(8,128)S(1)}, f32[1,256,256]{2,1,0:T(8,128)S(1)}, u32[]{:S(2)}, u32[]{:S(2)}) collective-permute-start(f32[1,256,256]{2,1,0:T(8,128)S(1)} %get-tuple-element.13), channel_id=1, source_target_pairs={{0,1},{1,2},{2,3},{3,4},{4,5},{5,6},{6,7},{8,9},{9,10},{10,11},{11... | collective-permute-start | bytes 786440 | tf_op jit(solution)/shard_map/ppermute | solution.py:39
  106.3 10.0 %collective-permute-start.7 = (f32[1,256,256]{2,1,0:T(8,128)S(1)}, f32[1,256,256]{2,1,0:T(8,128)S(1)}, u32[]{:S(2)}, u32[]{:S(2)}) collective-permute-start(f32[1,256,256]{2,1,0:T(8,128)S(1)} %get-tuple-element.14), channel_id=1, source_target_pairs={{8,0},{16,8},{24,16},{9,1},{17,9},{25,17},{10,2},{18,10},{26,18},{... | collective-permute-start | bytes 786440 | tf_op jit(solution)/shard_map/ppermute | solution.py:40
  107.6 10.1 %collective-permute-start.6 = (f32[1,256,256]{2,1,0:T(8,128)S(1)}, f32[1,256,256]{2,1,0:T(8,128)S(1)}, u32[]{:S(2)}, u32[]{:S(2)}) collective-permute-start(f32[1,256,256]{2,1,0:T(8,128)S(1)} %get-tuple-element.15), channel_id=1, source_target_pairs={{0,8},{8,16},{16,24},{1,9},{9,17},{17,25},{2,10},{10,18},{18,26},{... | collective-permute-start | bytes 786440 | tf_op jit(solution)/shard_map/ppermute | solution.py:39
  112.2 9.9 %collective-permute-start.5 = (f32[1,256,256]{2,1,0:T(8,128)S(1)}, f32[1,256,256]{2,1,0:T(8,128)S(1)}, u32[]{:S(2)}, u32[]{:S(2)}) collective-permute-start(f32[1,256,256]{2,1,0:T(8,128)S(1)} %get-tuple-element.16), channel_id=1, source_target_pairs={{1,0},{2,1},{3,2},{4,3},{5,4},{6,5},{7,6},{9,8},{10,9},{11,10},{12... | collective-permute-start | bytes 786440 | tf_op jit(solution)/shard_map/ppermute | solution.py:40
  170.9 9.4 %collective-permute-start.15 = (f32[1,256,256]{2,1,0:T(8,128)S(1)}, f32[1,256,256]{2,1,0:T(8,128)S(1)}, u32[]{:S(2)}, u32[]{:S(2)}) collective-permute-start(f32[1,256,256]{2,1,0:T(8,128)S(1)} %get-tuple-element.9), channel_id=1, source_target_pairs={{0,1},{1,2},{2,3},{3,4},{4,5},{5,6},{6,7},{8,9},{9,10},{10,11},{11... | collective-permute-start | bytes 786440 | tf_op jit(solution)/shard_map/ppermute | solution.py:39
  174.1 7.4 %collective-permute-start.17 = (f32[1,256,256]{2,1,0:T(8,128)S(1)}, f32[1,256,256]{2,1,0:T(8,128)S(1)}, u32[]{:S(2)}, u32[]{:S(2)}) collective-permute-start(f32[1,256,256]{2,1,0:T(8,128)S(1)} %get-tuple-element.10), channel_id=1, source_target_pairs={{0,8},{8,16},{16,24},{1,9},{9,17},{17,25},{2,10},{10,18},{18,26},{... | collective-permute-start | bytes 786440 | tf_op jit(solution)/shard_map/ppermute | solution.py:39
  177.5 8.3 %collective-permute-start.16 = (f32[1,256,256]{2,1,0:T(8,128)S(1)}, f32[1,256,256]{2,1,0:T(8,128)S(1)}, u32[]{:S(2)}, u32[]{:S(2)}) collective-permute-start(f32[1,256,256]{2,1,0:T(8,128)S(1)} %get-tuple-element.11), channel_id=1, source_target_pairs={{1,0},{2,1},{3,2},{4,3},{5,4},{6,5},{7,6},{9,8},{10,9},{11,10},{12... | collective-permute-start | bytes 786440 | tf_op jit(solution)/shard_map/ppermute | solution.py:40
  178.8 8.6 %collective-permute-start.18 = (f32[1,256,256]{2,1,0:T(8,128)S(1)}, f32[1,256,256]{2,1,0:T(8,128)S(1)}, u32[]{:S(2)}, u32[]{:S(2)}) collective-permute-start(f32[1,256,256]{2,1,0:T(8,128)S(1)} %get-tuple-element.12), channel_id=1, source_target_pairs={{8,0},{16,8},{24,16},{9,1},{17,9},{25,17},{10,2},{18,10},{26,18},{... | collective-permute-start | bytes 786440 | tf_op jit(solution)/shard_map/ppermute | solution.py:40
  198.6 6.7 %collective-permute-start.23 = (bf16[64,256]{1,0:T(8,128)(2,1)S(1)}, bf16[64,256]{1,0:T(8,128)(2,1)S(1)}, u32[]{:S(2)}, u32[]{:S(2)}) collective-permute-start(bf16[64,256]{1,0:T(8,128)(2,1)S(1)} %convolution_convert_fusion.3), channel_id=1, source_target_pairs={{0,1},{1,2},{2,3},{3,4},{4,5},{5,6},{6,7},{7,0},{8,9},{9,10},{10,1... | collective-permute-start | bytes 98312 | tf_op jit(solution)/shard_map/ppermute | solution.py:23
  211.9 6.8 %collective-permute-start.25 = (bf16[64,256]{1,0:T(8,128)(2,1)S(1)}, bf16[64,256]{1,0:T(8,128)(2,1)S(1)}, u32[]{:S(2)}, u32[]{:S(2)}) collective-permute-start(bf16[64,256]{1,0:T(8,128)(2,1)S(1)} %collective-permute-done.24), channel_id=1, source_target_pairs={{0,1},{1,2},{2,3},{3,4},{4,5},{5,6},{6,7},{7,0},{8,9},{9,10},{10,1... | collective-permute-start | bytes 98312 | tf_op jit(solution)/shard_map/ppermute | solution.py:23
  211.9 6.8 %collective-permute-start.28 = (bf16[64,256]{1,0:T(8,128)(2,1)S(1)}, bf16[64,256]{1,0:T(8,128)(2,1)S(1)}, u32[]{:S(2)}, u32[]{:S(2)}) collective-permute-start(bf16[64,256]{1,0:T(8,128)(2,1)S(1)} %collective-permute-done.27), channel_id=1, source_target_pairs={{1,0},{2,1},{3,2},{4,3},{5,4},{6,5},{7,6},{0,7},{9,8},{10,9},{11,1... | collective-permute-start | bytes 98312 | tf_op jit(solution)/shard_map/ppermute | solution.py:25
  226.8 83.2 %reduce-scatter.9.cloned.1.call-start = ((), (), s32[]{:S(2)}) async-start(), calls=%async_computation.5 | async-start | bytes 589824
  254.7 10.5 %collective-permute-start.19 = (f32[1,256,256]{2,1,0:T(8,128)S(1)}, f32[1,256,256]{2,1,0:T(8,128)S(1)}, u32[]{:S(2)}, u32[]{:S(2)}) collective-permute-start(f32[1,256,256]{2,1,0:T(8,128)S(1)} %get-tuple-element.5), channel_id=1, source_target_pairs={{0,1},{1,2},{2,3},{3,4},{4,5},{5,6},{6,7},{8,9},{9,10},{10,11},{11... | collective-permute-start | bytes 786440 | tf_op jit(solution)/shard_map/ppermute | solution.py:39
  258.0 10.1 %collective-permute-start.22 = (f32[1,256,256]{2,1,0:T(8,128)S(1)}, f32[1,256,256]{2,1,0:T(8,128)S(1)}, u32[]{:S(2)}, u32[]{:S(2)}) collective-permute-start(f32[1,256,256]{2,1,0:T(8,128)S(1)} %get-tuple-element.6), channel_id=1, source_target_pairs={{8,0},{16,8},{24,16},{9,1},{17,9},{25,17},{10,2},{18,10},{26,18},{... | collective-permute-start | bytes 786440 | tf_op jit(solution)/shard_map/ppermute | solution.py:40
  259.3 10.1 %collective-permute-start.21 = (f32[1,256,256]{2,1,0:T(8,128)S(1)}, f32[1,256,256]{2,1,0:T(8,128)S(1)}, u32[]{:S(2)}, u32[]{:S(2)}) collective-permute-start(f32[1,256,256]{2,1,0:T(8,128)S(1)} %get-tuple-element.7), channel_id=1, source_target_pairs={{0,8},{8,16},{16,24},{1,9},{9,17},{17,25},{2,10},{10,18},{18,26},{... | collective-permute-start | bytes 786440 | tf_op jit(solution)/shard_map/ppermute | solution.py:39
  263.9 9.9 %collective-permute-start.20 = (f32[1,256,256]{2,1,0:T(8,128)S(1)}, f32[1,256,256]{2,1,0:T(8,128)S(1)}, u32[]{:S(2)}, u32[]{:S(2)}) collective-permute-start(f32[1,256,256]{2,1,0:T(8,128)S(1)} %get-tuple-element.8), channel_id=1, source_target_pairs={{1,0},{2,1},{3,2},{4,3},{5,4},{6,5},{7,6},{9,8},{10,9},{11,10},{12... | collective-permute-start | bytes 786440 | tf_op jit(solution)/shard_map/ppermute | solution.py:40
  (17 other events, 194.1 us)
Sparse Core Ops, SparseCore 0:
  74.9 17.2 all-gather.2
  95.6 62.8 reduce-scatter.6
  226.9 17.0 all-gather.4
  247.2 62.7 reduce-scatter.8
